TPU v7x, 32 devices: a whole 2x2x4 slice. The times are simulated.
32 devices in a mesh: group: 4 (over z), expert: 8 (over y, x, core).
Axes of the slice: x: 2, y: 2, z: 4, core: 2. Of those that a mesh axis runs over, the one named last changes fastest.
Arguments:
- group_logits: float32 [4096, 4], P(('group', 'expert')), may hold values from -6 to 6
- expert_logits: float32 [4096, 32], P(('group', 'expert')), may hold values from -6 to 6
- expert_ids: int32 [4096, 2], P(('group', 'expert')), may hold values from 0 to 31, all different within a row; in each aligned block of 128 rows (0 to 127, 128 to 255, ...) at most 16 rows name the same one
- cotangent: bfloat16 [4096, 3584], P(('group', 'expert')), may hold values from -6 to 6
- hidden_saved: bfloat16 [32, 512, 1024], P(('group', 'expert')), may hold values from -0.1875 to 0.1875
- w_down: bfloat16 [32, 1024, 3584], P(('group', 'expert')), may hold values from -0.1875 to 0.1875
Outputs:
- hidden_grad: bfloat16 [32, 512, 1024], P(('group', 'expert'))
- d_group_logits: float32 [4096, 4], P(('group', 'expert'))
- d_expert_logits: float32 [4096, 32], P(('group', 'expert'))
Inputs may be any that keep to these rules, and one draw needn't show every extreme that they name: `expert_ids`: within the 128 tokens of one device no expert is named by more than 16 choices, a bound that some block reaches; the 2 experts of a token differ.
All inputs are finite; a program needn't handle non-finite values.
Results may differ from a plain program's by a relative error of at most 0.0045.
Values may be sent and summed in bfloat16 or wider, within the bound.
No kernel may reach another device: no remote copies, remote signals or barrier semaphores. Data moves between devices by JAX's collectives and lax.ppermute only.
A program may use at most 64 MiB of HBM per device.

v0:
```python
from functools import partial
import jax
import jax.numpy as jnp
from jax import lax
from jax.sharding import PartitionSpec as P

ITERS = 5
SOFTCAP = 4.0


def capped(logits):
    return jnp.exp(SOFTCAP * jnp.tanh(logits / SOFTCAP))


def squashing(logits):
    bounded = jnp.tanh(logits / SOFTCAP)
    return 1.0 - bounded * bounded


def balance_level(level_in, target, column_sum):
    scaled = level_in * (target / column_sum)
    return (scaled, jnp.sum(scaled, -1, keepdims=True))


def adjoint_local(out_grad, level_in, target, column_sum):
    scaled, row_total = balance_level(level_in, target, column_sum)
    level_out = scaled / row_total
    scaled_grad = (out_grad - jnp.sum(out_grad * level_out, -1, keepdims=True)) / row_total
    return (scaled_grad, jnp.sum(scaled_grad * level_in, 0))


def adjoint_finish(scaled_grad, inner, target, column_sum):
    return target / column_sum * (scaled_grad - inner / column_sum)


def balance_step(targets, current, unused):
    target_group, target_expert = targets
    group_in, expert_in = current
    group_cols, expert_cols = lax.psum(
        (jnp.sum(group_in, 0), jnp.sum(expert_in, 0)), ("group", "expert")
    )
    scaled_g, rowsum_g = balance_level(group_in, target_group, group_cols)
    scaled_e, rowsum_e = balance_level(expert_in, target_expert, expert_cols)
    return (
        (scaled_g / rowsum_g, scaled_e / rowsum_e),
        (group_in, expert_in, group_cols, expert_cols),
    )


def adjoint_step(targets, carried, stored_step):
    target_group, target_expert = targets
    grad_g, grad_e = carried
    group_in, expert_in, group_cols, expert_cols = stored_step
    scaled_g, inner_g = adjoint_local(grad_g, group_in, target_group, group_cols)
    scaled_e, inner_e = adjoint_local(grad_e, expert_in, target_expert, expert_cols)
    inner_g, inner_e = lax.psum((inner_g, inner_e), ("group", "expert"))
    next_g = adjoint_finish(scaled_g, inner_g, target_group, group_cols)
    next_e = adjoint_finish(scaled_e, inner_e, target_expert, expert_cols)
    return ((next_g, next_e), None)


def deliver(payload):
    halfway = (
        lax.all_to_all(payload[0], "expert", split_axis=1, concat_axis=1, tiled=True),
        lax.all_to_all(payload[1], "expert", split_axis=1, concat_axis=1, tiled=True),
    )
    return (
        lax.all_to_all(halfway[0], "group", split_axis=0, concat_axis=0, tiled=True),
        lax.all_to_all(halfway[1], "group", split_axis=0, concat_axis=0, tiled=True),
    )


def per_device(group_logits, expert_logits, expert_ids, cotangent, hidden_saved, w_down):
    groups = lax.axis_size("group")
    per_group = lax.axis_size("expert")
    experts = groups * per_group
    tokens_here = cotangent.shape[0]
    top_count = expert_ids.shape[1]
    model_width = cotangent.shape[1]
    capacity = hidden_saved.shape[1] // experts
    targets = (float(tokens_here * per_group), float(tokens_here * groups))
    flat_ids = expert_ids.reshape(-1)
    picked = (flat_ids[:, None] == jnp.arange(experts, dtype=jnp.int32)[None, :]).astype(jnp.int32)
    positions = jnp.sum((jnp.cumsum(picked, 0) - picked) * picked, 1)
    slot_index = flat_ids * capacity + positions
    serial = jnp.arange(flat_ids.shape[0], dtype=jnp.int32)
    source_index = jnp.zeros((experts * capacity,), jnp.int32).at[slot_index].set(serial)
    filled = jnp.zeros((experts * capacity,), jnp.int32).at[slot_index].set(1)
    fetched = jnp.take(cotangent, source_index // top_count, axis=0)
    send_rows = jnp.where(filled[:, None] > 0, fetched, jnp.zeros_like(fetched))
    send_rows = send_rows.reshape(groups, per_group, capacity, model_width)
    group_of = expert_ids // per_group
    group_aff = capped(group_logits)
    expert_aff = capped(expert_logits).reshape(tokens_here, groups, per_group)
    (group_prob, expert_prob), stored = lax.scan(
        partial(balance_step, targets), (group_aff, expert_aff), None, length=ITERS
    )
    pick_group = jnp.take_along_axis(group_prob, group_of, 1)
    pick_expert = jnp.take_along_axis(expert_prob.reshape(tokens_here, experts), expert_ids, 1)
    pair_prob = pick_group * pick_expert
    total_prob = jnp.sum(pair_prob, 1, keepdims=True)
    gate_prob = pair_prob / total_prob
    gate_sent = (
        jnp.zeros((experts * capacity,), jnp.bfloat16)
        .at[slot_index]
        .set(gate_prob.astype(jnp.bfloat16).reshape(-1))
    )
    gate_sent = gate_sent.reshape(groups, per_group, capacity)
    routed = (
        group_aff,
        expert_aff,
        stored,
        pick_group,
        pick_expert,
        total_prob,
        gate_prob,
        gate_sent,
    )
    got_rows, got_gates = deliver((send_rows, routed[7]))
    group_aff, expert_aff, stored, pick_group, pick_expert, total_prob, gate_prob, unused_gates = (
        routed
    )
    weight = w_down[0]
    saved_hidden = hidden_saved[0]
    expert_rows = got_rows.reshape(-1, model_width)
    unscaled = lax.dot_general(
        expert_rows, weight, (((1,), (1,)), ((), ())), preferred_element_type=jnp.float32
    )
    slot_grad = jnp.sum(unscaled * saved_hidden.astype(jnp.float32), 1)
    grad_rows = (got_gates.reshape(-1, 1).astype(jnp.float32) * unscaled).astype(jnp.bfloat16)
    hidden_grad = grad_rows[None]
    answers = lax.all_to_all(
        lax.all_to_all(
            slot_grad.reshape(groups, per_group, capacity),
            "group",
            split_axis=0,
            concat_axis=0,
            tiled=True,
        ),
        "expert",
        split_axis=1,
        concat_axis=1,
        tiled=True,
    )
    gate_grad = answers.reshape(-1)[slot_index].reshape(tokens_here, top_count)
    pair_grad = (gate_grad - jnp.sum(gate_prob * gate_grad, 1, keepdims=True)) / total_prob
    group_pick = (
        group_of[:, :, None] == jnp.arange(groups, dtype=jnp.int32)[None, None, :]
    ).astype(jnp.float32)
    seed_group = jnp.sum(group_pick * (pair_grad * pick_expert)[:, :, None], 1)
    expert_pick = (
        expert_ids[:, :, None] == jnp.arange(experts, dtype=jnp.int32)[None, None, :]
    ).astype(jnp.float32)
    seed_expert = jnp.sum(expert_pick * (pair_grad * pick_group)[:, :, None], 1).reshape(
        tokens_here, groups, per_group
    )
    (grad_group, grad_expert), unused = lax.scan(
        partial(adjoint_step, targets), (seed_group, seed_expert), stored, reverse=True
    )
    d_group_logits = grad_group * group_aff * squashing(group_logits)
    d_expert_logits = (grad_expert * expert_aff).reshape(tokens_here, experts) * squashing(
        expert_logits
    )
    return (hidden_grad, d_group_logits, d_expert_logits)


def solution(mesh):
    in_specs = (
        P(("group", "expert"), None),
        P(("group", "expert"), None),
        P(("group", "expert"), None),
        P(("group", "expert"), None),
        P(("group", "expert"), None, None),
        P(("group", "expert"), None, None),
    )
    out_specs = (
        P(("group", "expert"), None, None),
        P(("group", "expert"), None),
        P(("group", "expert"), None),
    )
    return jax.shard_map(
        per_device, mesh=mesh, in_specs=in_specs, out_specs=out_specs, check_vma=False
    )
```

profile of v0, /device:TPU:0, one launch (start us, length us, event | category | flops | bytes accessed | tf_op | source)
XLA Modules:
  0.0 600.4 jit_solution(14312915412681843163)
XLA Ops:
  5.2 1.4 scatter_custom_fusion.1
  6.8 4.2 gather_fusion
  10.9 3.6 fusion.16
  14.6 5.3 all-to-all-start.2
  20.3 43.2 %all-to-all-done.2 = bf16[4,8,16,3584]{3,2,0,1:T(8,128)(2,1)} async-done(((bf16[4,8,16,3584]{3,2,0,1:T(8,128)(2,1)}), bf16[4,8,16,3584]{3,2,0,1:T(8,128)(2,1)}, u32[]{:S(2)}, u32[]{:S(2)}) %all-to-all-start.2) | async-done | bytes 3670048 | tf_op jit(solution)/shard_map/all_to_all | solution.py:64
  63.5 4.2 copy.114
  67.6 5.6 all-to-all-start.3
  73.2 264.1 %while.36 = (s32[]{:T(128)}, f32[128,4]{0,1:T(4,128)S(1)}, f32[128,4,8]{0,2,1:T(8,128)S(1)}, f32[5,128,4]{1,2,0:T(4,128)S(1)}, f32[5,128,4,8]{1,3,2,0:T(8,128)S(...) while((s32[]{:T(128)}, f32[128,4]{0,1:T(4,128)S(1)}, ...), condition=%wide.region_10.11_spmd, body=%wide.region_3.10_spmd.sunk | while | flops 15277 | bytes 133133 | solution.py:95
  73.4 100.2 %all-reduce.4 = (f32[4]{0:T(128)S(1)}, f32[4,8]{1,0:T(4,128)S(1)}) all-reduce(f32[4]{0:T(128)S(1)} %reduce_sum.212, f32[4,8]{1,0:T(4,128)S(1)} %reduce_sum.213), channel_id=1, replica_groups=mesh['group'=4,'expert'=8] {'group','expert'}, use_global_device_ids=true, to_apply=%region_5.5 | all-reduce | flops 36 | bytes 288 | tf_op jit(solution)/shard_map/while/body/eval_jaxpr/psum | solution.py:39
  174.4 39.5 %all-reduce.4 = (f32[4]{0:T(128)S(1)}, f32[4,8]{1,0:T(4,128)S(1)}) all-reduce(f32[4]{0:T(128)S(1)} %reduce_sum.212, f32[4,8]{1,0:T(4,128)S(1)} %reduce_sum.213), channel_id=1, replica_groups=mesh['group'=4,'expert'=8] {'group','expert'}, use_global_device_ids=true, to_apply=%region_5.5 | all-reduce | flops 36 | bytes 288 | tf_op jit(solution)/shard_map/while/body/eval_jaxpr/psum | solution.py:39
  214.7 40.5 %all-reduce.4 = (f32[4]{0:T(128)S(1)}, f32[4,8]{1,0:T(4,128)S(1)}) all-reduce(f32[4]{0:T(128)S(1)} %reduce_sum.212, f32[4,8]{1,0:T(4,128)S(1)} %reduce_sum.213), channel_id=1, replica_groups=mesh['group'=4,'expert'=8] {'group','expert'}, use_global_device_ids=true, to_apply=%region_5.5 | all-reduce | flops 36 | bytes 288 | tf_op jit(solution)/shard_map/while/body/eval_jaxpr/psum | solution.py:39
  256.0 39.4 %all-reduce.4 = (f32[4]{0:T(128)S(1)}, f32[4,8]{1,0:T(4,128)S(1)}) all-reduce(f32[4]{0:T(128)S(1)} %reduce_sum.212, f32[4,8]{1,0:T(4,128)S(1)} %reduce_sum.213), channel_id=1, replica_groups=mesh['group'=4,'expert'=8] {'group','expert'}, use_global_device_ids=true, to_apply=%region_5.5 | all-reduce | flops 36 | bytes 288 | tf_op jit(solution)/shard_map/while/body/eval_jaxpr/psum | solution.py:39
  296.1 40.6 %all-reduce.4 = (f32[4]{0:T(128)S(1)}, f32[4,8]{1,0:T(4,128)S(1)}) all-reduce(f32[4]{0:T(128)S(1)} %reduce_sum.212, f32[4,8]{1,0:T(4,128)S(1)} %reduce_sum.213), channel_id=1, replica_groups=mesh['group'=4,'expert'=8] {'group','expert'}, use_global_device_ids=true, to_apply=%region_5.5 | all-reduce | flops 36 | bytes 288 | tf_op jit(solution)/shard_map/while/body/eval_jaxpr/psum | solution.py:39
  337.3 2.4 gather_fusion.2
  340.1 2.0 gather_fusion.3
  342.3 8.4 %fusion.17 = (f32[512]{0:T(512)S(1)}, f32[512,1024]{1,0:T(8,128)S(1)}) fusion(bf16[1,512,1024]{2,1,0:T(8,128)(2,1)} %param.14, bf16[512,3584]{1,0:T(8,128)(2,1)} %bitcast.18, bf16[1,1024,3584]{2,1,0:T(8,128)(2,1)} %param.15), kind=kOutput, calls=%fused_computation.49 | convolution fusion | flops 3759668736 | bytes 14157824 | tf_op jit(solution)/shard_map/dot_general | solution.py:126
  351.5 3.4 all-to-all-start.4
  354.9 5.5 all-to-all-done.4
  362.2 4.6 all-to-all-start.5
  366.9 4.7 all-to-all-done.5
  371.7 2.0 gather_fusion.1
  373.9 204.3 %while.37 = (s32[]{:T(128)}, f32[128,4]{0,1:T(4,128)S(1)}, f32[128,4,8]{0,2,1:T(8,128)S(1)}, f32[5,4]{1,0:T(8,128)S(1)}, f32[5,128,4]{1,2,0:T(4,128)S(1)}, /*ind...) while((s32[]{:T(128)}, f32[128,4]{0,1:T(4,128)S(1)}, ...), condition=%wide.region_28.29_spmd, body=%wide.region_19.28_spmd.sunk | while | flops 52050 | bytes 159945 | solution.py:157
  375.0 38.3 %all-reduce.5 = (f32[4]{0:T(128)S(1)}, f32[4,8]{1,0:T(4,128)S(1)}) all-reduce(f32[4]{0:T(128)S(1)} %fusion.48, f32[4,8]{1,0:T(4,128)S(1)} %get-tuple-element.338), channel_id=1, replica_groups=mesh['group'=4,'expert'=8] {'group','expert'}, use_global_device_ids=true, to_apply=%region_23.23 | all-reduce | flops 36 | bytes 288 | tf_op jit(solution)/shard_map/while/body/eval_jaxpr/psum | solution.py:56
  414.5 40.1 %all-reduce.5 = (f32[4]{0:T(128)S(1)}, f32[4,8]{1,0:T(4,128)S(1)}) all-reduce(f32[4]{0:T(128)S(1)} %fusion.48, f32[4,8]{1,0:T(4,128)S(1)} %get-tuple-element.338), channel_id=1, replica_groups=mesh['group'=4,'expert'=8] {'group','expert'}, use_global_device_ids=true, to_apply=%region_23.23 | all-reduce | flops 36 | bytes 288 | tf_op jit(solution)/shard_map/while/body/eval_jaxpr/psum | solution.py:56
  455.8 39.9 %all-reduce.5 = (f32[4]{0:T(128)S(1)}, f32[4,8]{1,0:T(4,128)S(1)}) all-reduce(f32[4]{0:T(128)S(1)} %fusion.48, f32[4,8]{1,0:T(4,128)S(1)} %get-tuple-element.338), channel_id=1, replica_groups=mesh['group'=4,'expert'=8] {'group','expert'}, use_global_device_ids=true, to_apply=%region_23.23 | all-reduce | flops 36 | bytes 288 | tf_op jit(solution)/shard_map/while/body/eval_jaxpr/psum | solution.py:56
  496.9 40.1 %all-reduce.5 = (f32[4]{0:T(128)S(1)}, f32[4,8]{1,0:T(4,128)S(1)}) all-reduce(f32[4]{0:T(128)S(1)} %fusion.48, f32[4,8]{1,0:T(4,128)S(1)} %get-tuple-element.338), channel_id=1, replica_groups=mesh['group'=4,'expert'=8] {'group','expert'}, use_global_device_ids=true, to_apply=%region_23.23 | all-reduce | flops 36 | bytes 288 | tf_op jit(solution)/shard_map/while/body/eval_jaxpr/psum | solution.py:56
  538.3 39.8 %all-reduce.5 = (f32[4]{0:T(128)S(1)}, f32[4,8]{1,0:T(4,128)S(1)}) all-reduce(f32[4]{0:T(128)S(1)} %fusion.48, f32[4,8]{1,0:T(4,128)S(1)} %get-tuple-element.338), channel_id=1, replica_groups=mesh['group'=4,'expert'=8] {'group','expert'}, use_global_device_ids=true, to_apply=%region_23.23 | all-reduce | flops 36 | bytes 288 | tf_op jit(solution)/shard_map/while/body/eval_jaxpr/psum | solution.py:56
  578.6 2.2 scatter_custom_fusion
  581.5 3.6 all-to-all-start
  585.6 4.1 all-to-all-done
  590.3 3.2 all-to-all-start.1
  594.2 5.0 all-to-all-done.1
  (188 shorter events, 22.5 us)
Async XLA Ops:
  0.6 6.1 %copy-start = (bf16[128,3584]{1,0:T(8,128)(2,1)S(1)}, bf16[128,3584]{1,0:T(8,128)(2,1)}, u32[]{:S(2)}) copy-start(bf16[128,3584]{1,0:T(8,128)(2,1)} %param.13) | copy-start | bytes 2752516
  14.6 5.4 copy-start.2
  14.6 5.7 copy-start.3
  14.6 5.7 copy-start.1
  14.6 48.9 %all-to-all-start.2 = ((bf16[4,8,16,3584]{3,2,0,1:T(8,128)(2,1)}), bf16[4,8,16,3584]{3,2,0,1:T(8,128)(2,1)}, u32[]{:S(2)}, u32[]{:S(2)}) async-start(bf16[4,8,16,3584]{3,2,0,1:T(8,128)(2,1)} %fusion.16), calls=%async_computation.2 | async-start | bytes 7340032 | tf_op jit(solution)/shard_map/all_to_all | solution.py:64
  67.6 274.7 %all-to-all-start.3 = ((bf16[4,8,16,3584]{3,2,1,0:T(8,128)(2,1)}), bf16[4,8,16,3584]{3,2,1,0:T(8,128)(2,1)}, u32[]{:S(2)}, u32[]{:S(2)}) async-start(bf16[4,8,16,3584]{3,2,1,0:T(8,128)(2,1)} %copy.114), calls=%async_computation.3 | async-start | bytes 7340032 | tf_op jit(solution)/shard_map/all_to_all | solution.py:68
  351.5 8.9 %all-to-all-start.4 = ((f32[4,1,128]{2,1,0:T(1,128)}), f32[4,1,128]{2,1,0:T(1,128)S(1)}, u32[]{:S(2)}, u32[]{:S(2)}) async-start(f32[4,1,128]{2,1,0:T(1,128)} %reshape.275), calls=%async_computation.4 | async-start | bytes 4096 | tf_op jit(solution)/shard_map/all_to_all | solution.py:133
  362.2 9.4 %all-to-all-start.5 = ((f32[4,8,16]{2,0,1:T(4,128)}), f32[4,8,16]{2,0,1:T(4,128)S(1)}, u32[]{:S(2)}, u32[]{:S(2)}) async-start(f32[4,8,16]{2,0,1:T(4,128)} %copy.115), calls=%async_computation.5 | async-start | bytes 32768 | tf_op jit(solution)/shard_map/all_to_all | solution.py:132
  581.5 8.3 %all-to-all-start = ((bf16[4,8,16]{2,0,1:T(4,128)(2,1)}), bf16[4,8,16]{2,0,1:T(4,128)(2,1)S(1)}, u32[]{:S(2)}, u32[]{:S(2)}) async-start(bf16[4,8,16]{2,0,1:T(4,128)(2,1)} %copy.109), calls=%async_computation | async-start | bytes 16384 | tf_op jit(solution)/shard_map/all_to_all | solution.py:65
  590.3 8.8 %all-to-all-start.1 = ((bf16[4,8,16]{2,1,0:T(8,128)(2,1)}), bf16[4,8,16]{2,1,0:T(8,128)(2,1)S(1)}, u32[]{:S(2)}, u32[]{:S(2)}) async-start(bf16[4,8,16]{2,1,0:T(8,128)(2,1)} %copy.110), calls=%async_computation.1 | async-start | bytes 16384 | tf_op jit(solution)/shard_map/all_to_all | solution.py:69
where the time goes:
time: 602 us; the launch traced here: 600 us
  blocking collectives  458 us (76%)
  waiting for transfers between devices  62.5 us (10%)
  local copies, waits for them, and re-layouts  26.5 us (4%)
  starting transfers between devices  25.7 us (4%)
  other arithmetic  17.9 us (3%)
  matrix products  8.44 us (1%)
    psum x5, blocking collectives, balance_step(): lax.psum((jnp.sum(group_in, 0), jnp.sum(expert_in, 0)), ('group', 'expert'))  260 us
    psum x5, blocking collectives, adjoint_step(): inner_g, inner_e = lax.psum((inner_g, inner_e), ('group', 'expert'))  198 us
    all_to_all x1, waiting for transfers between devices, deliver(): lax.all_to_all(payload[0], 'expert', split_axis=1, concat_axis=1, tiled=T...  43.2 us
  transfers between devices with their start and end apart: 6, of which 5 were waited for; matrix products, arithmetic and copies ran while one was open for 2% of the time, Pallas kernels for 0%

commit v1 on v0

--- a/solution.py
+++ b/solution.py
@@ -6,6 +6,29 @@
 
 ITERS = 5
 SOFTCAP = 4.0
+
+
+def in_blocks(x, dim, count):
+    before, after = (x.shape[:dim], x.shape[dim + 1 :])
+    return jnp.moveaxis(x.reshape(*before, count, -1, *after), dim, 0)
+
+
+def joined_along(parts, dim):
+    dims = list(parts.shape[1:])
+    dims[dim] *= parts.shape[0]
+    return jnp.moveaxis(parts, 0, dim).reshape(dims)
+
+
+def exchange_directly(array, axis, split_dim, concat_dim):
+    size, index = (lax.axis_size(axis), lax.axis_index(axis))
+    blocks = in_blocks(array, split_dim, size)
+    result = blocks
+    for turn in range(1, size):
+        target, source = ((index + turn) % size, (index - turn) % size)
+        sent = lax.dynamic_index_in_dim(blocks, target, 0)
+        partner_block = lax.ppermute(sent, axis, [(i, (i + turn) % size) for i in range(size)])
+        result = lax.dynamic_update_slice_in_dim(result, partner_block, source, axis=0)
+    return joined_along(result, concat_dim)
 
 
 def capped(logits):
@@ -61,7 +84,7 @@
 
 def deliver(payload):
     halfway = (
-        lax.all_to_all(payload[0], "expert", split_axis=1, concat_axis=1, tiled=True),
+        exchange_directly(payload[0], "expert", 1, 1),
         lax.all_to_all(payload[1], "expert", split_axis=1, concat_axis=1, tiled=True),
     )
     return (

time: 602 us -> 598 us (level)
  waiting for transfers between devices: 62.5 us -> 40 us
  starting transfers between devices: 25.7 us -> 36.7 us
    all_to_all x1 -> x0, waiting for transfers between devices: 43.2 us -> none  [deliver(): lax.all_to_all(payload[0], 'expert', split_axis=1, concat_axis=1, tiled=T...]
    ppermute x0 -> x7, waiting for transfers between devices: none -> 20.7 us  [exchange_directly(): lax.ppermute(sent, axis, [(i, (i + turn) % size) for i in range(size)])]
    ppermute x0 -> x7, starting transfers between devices: none -> 17.2 us  [exchange_directly(): lax.ppermute(sent, axis, [(i, (i + turn) % size) for i in range(size)])]
  transfers between devices with their start and end apart: 6 -> 12, of which waited for: 5 -> 7; matrix products, arithmetic and copies ran while one was open for 2% -> 3% of each run, Pallas kernels for 0% -> 0%
where the time goes in v1:
time: 598 us; the launch traced here: 596 us
  blocking collectives  461 us (77%)
  waiting for transfers between devices  40 us (7%)
  starting transfers between devices  36.7 us (6%)
  local copies, waits for them, and re-layouts  29.7 us (5%)
  other arithmetic  19.1 us (3%)
  matrix products  8.44 us (1%)
    psum x5, blocking collectives, balance_step(): lax.psum((jnp.sum(group_in, 0), jnp.sum(expert_in, 0)), ('group', 'expert'))  262 us
    psum x5, blocking collectives, adjoint_step(): inner_g, inner_e = lax.psum((inner_g, inner_e), ('group', 'expert'))  198 us
    ppermute x7, waiting for transfers between devices, exchange_directly(): lax.ppermute(sent, axis, [(i, (i + turn) % size) for i in range(size)])  20.7 us
    ppermute x7, starting transfers between devices, exchange_directly(): lax.ppermute(sent, axis, [(i, (i + turn) % size) for i in range(size)])  17.2 us
  transfers between devices with their start and end apart: 12, of which 7 were waited for; matrix products, arithmetic and copies ran while one was open for 3% of the time, Pallas kernels for 0%

profile of v1, /device:TPU:0, one launch (start us, length us, event | category | flops | bytes accessed | tf_op | source)
XLA Modules:
  0.0 595.9 jit_solution(8862308221108048610)
XLA Ops:
  6.7 4.2 gather_fusion
  10.9 2.6 select_select_fusion
  15.7 2.5 collective-permute-start.1
  18.1 2.4 collective-permute-start.2
  24.0 5.1 collective-permute-done
  29.0 2.5 collective-permute-start.5
  32.4 8.7 %collective-permute-start.6 = (bf16[1,4,1,16,3584]{4,3,0,1,2:T(8,128)(2,1)}, bf16[1,4,1,16,3584]{4,3,0,1,2:T(8,128)(2,1)S(1)}, u32[]{:S(2)}, u32[]{:S(2)}) collective-permute-start(bf16[1,4,1,16,3584]{4,3,0,1,2:T(8,128)(2,1)} %get-tuple-element.239), channel_id=1, source_target_pairs={{0,7},{1,0},{2,1},{3,2},{4,3},{5,4},{6,5},{7,6},{8,15},{9,8},{10,9... | collective-permute-start | bytes 1376264 | tf_op jit(solution)/shard_map/ppermute | solution.py:29
  41.9 7.5 %collective-permute-done.2 = bf16[1,4,1,16,3584]{4,3,0,1,2:T(8,128)(2,1)S(1)} collective-permute-done((bf16[1,4,1,16,3584]{4,3,0,1,2:T(8,128)(2,1)}, bf16[1,4,1,16,3584]{4,3,0,1,2:T(8,128)(2,1)S(1)}, u32[]{:S(2)}, u32[]{:S(2)}) %collective-permute-start.2) | collective-permute-done | bytes 458784 | tf_op jit(solution)/shard_map/ppermute | solution.py:29
  51.0 8.2 %collective-permute-done.4 = bf16[1,4,1,16,3584]{4,3,0,1,2:T(8,128)(2,1)S(1)} collective-permute-done((bf16[1,4,1,16,3584]{4,3,0,1,2:T(8,128)(2,1)}, bf16[1,4,1,16,3584]{4,3,0,1,2:T(8,128)(2,1)S(1)}, u32[]{:S(2)}, u32[]{:S(2)}) %collective-permute-start.4) | collective-permute-done | bytes 458784 | tf_op jit(solution)/shard_map/ppermute | solution.py:29
  61.7 4.9 all-to-all-start.2
  66.5 266.4 %while.36 = (s32[]{:T(128)}, f32[128,4]{0,1:T(4,128)S(1)}, f32[128,4,8]{0,2,1:T(8,128)S(1)}, f32[5,128,4]{1,2,0:T(4,128)S(1)}, f32[5,128,4,8]{1,3,2,0:T(8,128)S(...) while((s32[]{:T(128)}, f32[128,4]{0,1:T(4,128)S(1)}, ...), condition=%wide.region_10.11_spmd, body=%wide.region_3.10_spmd.sunk | while | flops 15277 | bytes 133133 | solution.py:118
  66.8 102.8 %all-reduce.4 = (f32[4]{0:T(128)S(1)}, f32[4,8]{1,0:T(4,128)S(1)}) all-reduce(f32[4]{0:T(128)S(1)} %reduce_sum.212, f32[4,8]{1,0:T(4,128)S(1)} %reduce_sum.213), channel_id=1, replica_groups=mesh['group'=4,'expert'=8] {'group','expert'}, use_global_device_ids=true, to_apply=%region_5.5 | all-reduce | flops 36 | bytes 288 | tf_op jit(solution)/shard_map/while/body/eval_jaxpr/psum | solution.py:62
  170.3 39.1 %all-reduce.4 = (f32[4]{0:T(128)S(1)}, f32[4,8]{1,0:T(4,128)S(1)}) all-reduce(f32[4]{0:T(128)S(1)} %reduce_sum.212, f32[4,8]{1,0:T(4,128)S(1)} %reduce_sum.213), channel_id=1, replica_groups=mesh['group'=4,'expert'=8] {'group','expert'}, use_global_device_ids=true, to_apply=%region_5.5 | all-reduce | flops 36 | bytes 288 | tf_op jit(solution)/shard_map/while/body/eval_jaxpr/psum | solution.py:62
  210.3 40.7 %all-reduce.4 = (f32[4]{0:T(128)S(1)}, f32[4,8]{1,0:T(4,128)S(1)}) all-reduce(f32[4]{0:T(128)S(1)} %reduce_sum.212, f32[4,8]{1,0:T(4,128)S(1)} %reduce_sum.213), channel_id=1, replica_groups=mesh['group'=4,'expert'=8] {'group','expert'}, use_global_device_ids=true, to_apply=%region_5.5 | all-reduce | flops 36 | bytes 288 | tf_op jit(solution)/shard_map/while/body/eval_jaxpr/psum | solution.py:62
  251.8 39.1 %all-reduce.4 = (f32[4]{0:T(128)S(1)}, f32[4,8]{1,0:T(4,128)S(1)}) all-reduce(f32[4]{0:T(128)S(1)} %reduce_sum.212, f32[4,8]{1,0:T(4,128)S(1)} %reduce_sum.213), channel_id=1, replica_groups=mesh['group'=4,'expert'=8] {'group','expert'}, use_global_device_ids=true, to_apply=%region_5.5 | all-reduce | flops 36 | bytes 288 | tf_op jit(solution)/shard_map/while/body/eval_jaxpr/psum | solution.py:62
  291.6 40.7 %all-reduce.4 = (f32[4]{0:T(128)S(1)}, f32[4,8]{1,0:T(4,128)S(1)}) all-reduce(f32[4]{0:T(128)S(1)} %reduce_sum.212, f32[4,8]{1,0:T(4,128)S(1)} %reduce_sum.213), channel_id=1, replica_groups=mesh['group'=4,'expert'=8] {'group','expert'}, use_global_device_ids=true, to_apply=%region_5.5 | all-reduce | flops 36 | bytes 288 | tf_op jit(solution)/shard_map/while/body/eval_jaxpr/psum | solution.py:62
  332.9 2.4 gather_fusion.2
  338.0 8.4 %fusion.16 = (f32[512]{0:T(512)S(1)}, f32[512,1024]{1,0:T(8,128)S(1)}) fusion(bf16[1,512,1024]{2,1,0:T(8,128)(2,1)} %param.14, bf16[512,3584]{1,0:T(8,128)(2,1)} %bitcast.28, bf16[1,1024,3584]{2,1,0:T(8,128)(2,1)} %param.15), kind=kOutput, calls=%fused_computation.48 | convolution fusion | flops 3759668736 | bytes 14157824 | tf_op jit(solution)/shard_map/dot_general | solution.py:149
  347.2 3.5 all-to-all-start.3
  350.8 5.5 all-to-all-done.3
  358.1 4.3 all-to-all-start.4
  362.4 4.7 all-to-all-done.4
  369.5 204.3 %while.37 = (s32[]{:T(128)}, f32[128,4]{0,1:T(4,128)S(1)}, f32[128,4,8]{0,2,1:T(8,128)S(1)}, f32[5,4]{1,0:T(8,128)S(1)}, f32[5,128,4]{1,2,0:T(4,128)S(1)}, /*ind...) while((s32[]{:T(128)}, f32[128,4]{0,1:T(4,128)S(1)}, ...), condition=%wide.region_28.29_spmd, body=%wide.region_19.28_spmd.sunk | while | flops 52050 | bytes 159945 | solution.py:180
  370.5 38.3 %all-reduce.5 = (f32[4]{0:T(128)S(1)}, f32[4,8]{1,0:T(4,128)S(1)}) all-reduce(f32[4]{0:T(128)S(1)} %fusion.48, f32[4,8]{1,0:T(4,128)S(1)} %get-tuple-element.346), channel_id=1, replica_groups=mesh['group'=4,'expert'=8] {'group','expert'}, use_global_device_ids=true, to_apply=%region_23.23 | all-reduce | flops 36 | bytes 288 | tf_op jit(solution)/shard_map/while/body/eval_jaxpr/psum | solution.py:79
  410.0 40.1 %all-reduce.5 = (f32[4]{0:T(128)S(1)}, f32[4,8]{1,0:T(4,128)S(1)}) all-reduce(f32[4]{0:T(128)S(1)} %fusion.48, f32[4,8]{1,0:T(4,128)S(1)} %get-tuple-element.346), channel_id=1, replica_groups=mesh['group'=4,'expert'=8] {'group','expert'}, use_global_device_ids=true, to_apply=%region_23.23 | all-reduce | flops 36 | bytes 288 | tf_op jit(solution)/shard_map/while/body/eval_jaxpr/psum | solution.py:79
  451.3 39.9 %all-reduce.5 = (f32[4]{0:T(128)S(1)}, f32[4,8]{1,0:T(4,128)S(1)}) all-reduce(f32[4]{0:T(128)S(1)} %fusion.48, f32[4,8]{1,0:T(4,128)S(1)} %get-tuple-element.346), channel_id=1, replica_groups=mesh['group'=4,'expert'=8] {'group','expert'}, use_global_device_ids=true, to_apply=%region_23.23 | all-reduce | flops 36 | bytes 288 | tf_op jit(solution)/shard_map/while/body/eval_jaxpr/psum | solution.py:79
  492.4 40.1 %all-reduce.5 = (f32[4]{0:T(128)S(1)}, f32[4,8]{1,0:T(4,128)S(1)}) all-reduce(f32[4]{0:T(128)S(1)} %fusion.48, f32[4,8]{1,0:T(4,128)S(1)} %get-tuple-element.346), channel_id=1, replica_groups=mesh['group'=4,'expert'=8] {'group','expert'}, use_global_device_ids=true, to_apply=%region_23.23 | all-reduce | flops 36 | bytes 288 | tf_op jit(solution)/shard_map/while/body/eval_jaxpr/psum | solution.py:79
  533.8 39.8 %all-reduce.5 = (f32[4]{0:T(128)S(1)}, f32[4,8]{1,0:T(4,128)S(1)}) all-reduce(f32[4]{0:T(128)S(1)} %fusion.48, f32[4,8]{1,0:T(4,128)S(1)} %get-tuple-element.346), channel_id=1, replica_groups=mesh['group'=4,'expert'=8] {'group','expert'}, use_global_device_ids=true, to_apply=%region_23.23 | all-reduce | flops 36 | bytes 288 | tf_op jit(solution)/shard_map/while/body/eval_jaxpr/psum | solution.py:79
  576.9 3.6 all-to-all-start
  581.1 4.1 all-to-all-done
  585.8 3.2 all-to-all-start.1
  589.7 5.0 all-to-all-done.1
  (207 shorter events, 40.8 us)
Async XLA Ops:
  0.6 6.1 %copy-start = (bf16[128,3584]{1,0:T(8,128)(2,1)S(1)}, bf16[128,3584]{1,0:T(8,128)(2,1)}, u32[]{:S(2)}) copy-start(bf16[128,3584]{1,0:T(8,128)(2,1)} %param.13) | copy-start | bytes 2752516
  13.4 7.7 %copy-start.1 = (bf16[512,3584]{1,0:T(8,128)(2,1)S(1)}, bf16[512,3584]{1,0:T(8,128)(2,1)}, u32[]{:S(2)}) copy-start(bf16[512,3584]{1,0:T(8,128)(2,1)} %gather_fusion) | copy-start | bytes 11010052
  15.2 13.9 %collective-permute-start = (bf16[1,4,1,16,3584]{4,3,0,1,2:T(8,128)(2,1)}, bf16[1,4,1,16,3584]{4,3,0,1,2:T(8,128)(2,1)S(1)}, u32[]{:S(2)}, u32[]{:S(2)}) collective-permute-start(bf16[1,4,1,16,3584]{4,3,0,1,2:T(8,128)(2,1)} %get-tuple-element.245), channel_id=1, source_target_pairs={{0,1},{1,2},{2,3},{3,4},{4,5},{5,6},{6,7},{7,0},{8,9},{9,10},{10,1... | collective-permute-start | bytes 1376264 | tf_op jit(solution)/shard_map/ppermute | solution.py:29
  15.7 16.7 %collective-permute-start.1 = (bf16[1,4,1,16,3584]{4,3,0,1,2:T(8,128)(2,1)}, bf16[1,4,1,16,3584]{4,3,0,1,2:T(8,128)(2,1)S(1)}, u32[]{:S(2)}, u32[]{:S(2)}) collective-permute-start(bf16[1,4,1,16,3584]{4,3,0,1,2:T(8,128)(2,1)} %get-tuple-element.244), channel_id=1, source_target_pairs={{0,2},{1,3},{2,4},{3,5},{4,6},{5,7},{6,0},{7,1},{8,10},{9,11},{10,... | collective-permute-start | bytes 1376264 | tf_op jit(solution)/shard_map/ppermute | solution.py:29
  18.1 31.2 %collective-permute-start.2 = (bf16[1,4,1,16,3584]{4,3,0,1,2:T(8,128)(2,1)}, bf16[1,4,1,16,3584]{4,3,0,1,2:T(8,128)(2,1)S(1)}, u32[]{:S(2)}, u32[]{:S(2)}) collective-permute-start(bf16[1,4,1,16,3584]{4,3,0,1,2:T(8,128)(2,1)} %get-tuple-element.243), channel_id=1, source_target_pairs={{0,3},{1,4},{2,5},{3,6},{4,7},{5,0},{6,1},{7,2},{8,11},{9,12},{10,... | collective-permute-start | bytes 1376264 | tf_op jit(solution)/shard_map/ppermute | solution.py:29
  20.6 29.6 %collective-permute-start.3 = (bf16[1,4,1,16,3584]{4,3,0,1,2:T(8,128)(2,1)}, bf16[1,4,1,16,3584]{4,3,0,1,2:T(8,128)(2,1)S(1)}, u32[]{:S(2)}, u32[]{:S(2)}) collective-permute-start(bf16[1,4,1,16,3584]{4,3,0,1,2:T(8,128)(2,1)} %get-tuple-element.242), channel_id=1, source_target_pairs={{0,4},{1,5},{2,6},{3,7},{4,0},{5,1},{6,2},{7,3},{8,12},{9,13},{10,... | collective-permute-start | bytes 1376264 | tf_op jit(solution)/shard_map/ppermute | solution.py:29
  21.1 2.4 copy-start.3
  21.1 2.9 copy-start.4
  21.1 2.9 copy-start.2
  21.1 38.1 %collective-permute-start.4 = (bf16[1,4,1,16,3584]{4,3,0,1,2:T(8,128)(2,1)}, bf16[1,4,1,16,3584]{4,3,0,1,2:T(8,128)(2,1)S(1)}, u32[]{:S(2)}, u32[]{:S(2)}) collective-permute-start(bf16[1,4,1,16,3584]{4,3,0,1,2:T(8,128)(2,1)} %get-tuple-element.241), channel_id=1, source_target_pairs={{0,5},{1,6},{2,7},{3,0},{4,1},{5,2},{6,3},{7,4},{8,13},{9,14},{10,... | collective-permute-start | bytes 1376264 | tf_op jit(solution)/shard_map/ppermute | solution.py:29
  29.0 31.0 %collective-permute-start.5 = (bf16[1,4,1,16,3584]{4,3,0,1,2:T(8,128)(2,1)}, bf16[1,4,1,16,3584]{4,3,0,1,2:T(8,128)(2,1)S(1)}, u32[]{:S(2)}, u32[]{:S(2)}) collective-permute-start(bf16[1,4,1,16,3584]{4,3,0,1,2:T(8,128)(2,1)} %get-tuple-element.240), channel_id=1, source_target_pairs={{0,6},{1,7},{2,0},{3,1},{4,2},{5,3},{6,4},{7,5},{8,14},{9,15},{10,... | collective-permute-start | bytes 1376264 | tf_op jit(solution)/shard_map/ppermute | solution.py:29
  32.4 28.5 %collective-permute-start.6 = (bf16[1,4,1,16,3584]{4,3,0,1,2:T(8,128)(2,1)}, bf16[1,4,1,16,3584]{4,3,0,1,2:T(8,128)(2,1)S(1)}, u32[]{:S(2)}, u32[]{:S(2)}) collective-permute-start(bf16[1,4,1,16,3584]{4,3,0,1,2:T(8,128)(2,1)} %get-tuple-element.239), channel_id=1, source_target_pairs={{0,7},{1,0},{2,1},{3,2},{4,3},{5,4},{6,5},{7,6},{8,15},{9,8},{10,9... | collective-permute-start | bytes 1376264 | tf_op jit(solution)/shard_map/ppermute | solution.py:29
  61.7 276.3 %all-to-all-start.2 = ((bf16[4,8,16,3584]{3,2,1,0:T(8,128)(2,1)}), bf16[4,8,16,3584]{3,2,1,0:T(8,128)(2,1)}, u32[]{:S(2)}, u32[]{:S(2)}) async-start(bf16[4,8,16,3584]{3,2,1,0:T(8,128)(2,1)} %bitcast.138), calls=%async_computation.2 | async-start | bytes 7340032 | tf_op jit(solution)/shard_map/all_to_all | solution.py:91
  347.2 9.0 %all-to-all-start.3 = ((f32[4,1,128]{2,1,0:T(1,128)}), f32[4,1,128]{2,1,0:T(1,128)S(1)}, u32[]{:S(2)}, u32[]{:S(2)}) async-start(f32[4,1,128]{2,1,0:T(1,128)} %reshape.301), calls=%async_computation.3 | async-start | bytes 4096 | tf_op jit(solution)/shard_map/all_to_all | solution.py:156
  358.1 9.0 %all-to-all-start.4 = ((f32[4,8,16]{2,0,1:T(4,128)}), f32[4,8,16]{2,0,1:T(4,128)S(1)}, u32[]{:S(2)}, u32[]{:S(2)}) async-start(f32[4,8,16]{2,0,1:T(4,128)} %copy.98), calls=%async_computation.4 | async-start | bytes 32768 | tf_op jit(solution)/shard_map/all_to_all | solution.py:155
  576.9 8.3 %all-to-all-start = ((bf16[4,8,16]{2,0,1:T(4,128)(2,1)}), bf16[4,8,16]{2,0,1:T(4,128)(2,1)S(1)}, u32[]{:S(2)}, u32[]{:S(2)}) async-start(bf16[4,8,16]{2,0,1:T(4,128)(2,1)} %copy.96), calls=%async_computation | async-start | bytes 16384 | tf_op jit(solution)/shard_map/all_to_all | solution.py:88
  585.8 8.8 %all-to-all-start.1 = ((bf16[4,8,16]{2,1,0:T(8,128)(2,1)}), bf16[4,8,16]{2,1,0:T(8,128)(2,1)S(1)}, u32[]{:S(2)}, u32[]{:S(2)}) async-start(bf16[4,8,16]{2,1,0:T(8,128)(2,1)} %copy.97), calls=%async_computation.1 | async-start | bytes 16384 | tf_op jit(solution)/shard_map/all_to_all | solution.py:92
